TPU v7x, 256 devices: a whole 4x4x8 slice. The times are simulated.
256 devices in a mesh: layer: 2 (over x_lo), row: 32 (over z, y), col: 4 (over x_hi, core).
Axes of the slice: x: 4 (x_hi: 2, x_lo: 2; x = x_hi * 2 + x_lo), y: 4, z: 8, core: 2. Of those that a mesh axis runs over, the one named last changes fastest.
Arguments:
- rhs_root: float32 [16384, 128], P('col'), may hold values from -6 to 6
- rhs_child: float32 [2, 8192, 128], P('layer', 'col'), may hold values from -6 to 6
- rhs_leaf: float32 [4, 4096, 128], P('layer', 'col'), may hold values from -6 to 6
- root_inv: bfloat16 [16384, 16384], P('row', 'col'), may hold values from -0.046875 to 0.046875
- child_inv: bfloat16 [2, 8192, 8192], P('layer', 'row', 'col'), may hold values from -0.0625 to 0.0625
- leaf_inv: bfloat16 [4, 4096, 4096], P('layer', 'row', 'col'), may hold values from -0.09375 to 0.09375
- leaf_to_child: bfloat16 [4, 8192, 4096], P('layer', 'col', 'row'), may hold values from -0.0625 to 0.0625
- leaf_to_root: bfloat16 [4, 16384, 4096], P('layer', 'col', 'row'), may hold values from -0.03125 to 0.03125
- child_to_root: bfloat16 [2, 16384, 8192], P('layer', 'col', 'row'), may hold values from -0.03125 to 0.03125
Outputs:
- x_root: float32 [16384, 128], P('col')
- x_child: float32 [2, 8192, 128], P('layer', 'col')
- x_leaf: float32 [4, 4096, 128], P('layer', 'col')
- y_root: float32 [16384, 128], P('row')
All inputs are finite; a program needn't handle non-finite values.
Results may differ from a plain program's by a relative error of at most 0.008.
Values sent between devices are 32-bit elements; how exact they have to be, the bound alone decides.
No kernel may reach another device: no remote copies, remote signals or barrier semaphores. Data moves between devices by JAX's collectives and lax.ppermute only.
A program may use at most 64 MiB of HBM per device.

v0:
```python
import jax
import jax.numpy as jnp
from jax import lax
from jax.sharding import PartitionSpec as P


def col_sum(values):
    return lax.psum(values, "col")


def row_sum(values):
    return lax.psum(values, "row")


def root_total(values):
    return lax.psum(values, ("layer", "row"))


def half16(values):
    return values.astype(jnp.bfloat16)


def on_device(
    rhs_root,
    rhs_child,
    rhs_leaf,
    root_inv,
    child_inv,
    leaf_inv,
    leaf_to_child,
    leaf_to_root,
    child_to_root,
):
    f32 = jnp.float32
    y_leaf = col_sum(
        jnp.einsum("gij,gjs->gis", leaf_inv, half16(rhs_leaf), preferred_element_type=f32)
    )
    leaf_bf = half16(y_leaf)
    leaf_update = jnp.einsum("gij,gjs->is", leaf_to_root, leaf_bf, preferred_element_type=f32)
    r_child = rhs_child[0] - row_sum(
        jnp.einsum("gij,gjs->is", leaf_to_child, leaf_bf, preferred_element_type=f32)
    )
    y_child = col_sum(jnp.dot(child_inv[0], half16(r_child), preferred_element_type=f32))
    child_update = jnp.dot(child_to_root[0], half16(y_child), preferred_element_type=f32)
    r_root = rhs_root - root_total(child_update + leaf_update)
    y_root = col_sum(jnp.dot(root_inv, half16(r_root), preferred_element_type=f32))
    x_root = row_sum(jnp.einsum("ij,is->js", root_inv, half16(y_root), preferred_element_type=f32))
    root_bf = half16(x_root)
    back_child = y_child - col_sum(
        jnp.einsum("ij,is->js", child_to_root[0], root_bf, preferred_element_type=f32)
    )
    x_child = row_sum(
        jnp.einsum("ij,is->js", child_inv[0], half16(back_child), preferred_element_type=f32)
    )
    terms = jnp.einsum("gij,is->gjs", leaf_to_child, half16(x_child), preferred_element_type=f32)
    terms = terms + jnp.einsum("gij,is->gjs", leaf_to_root, root_bf, preferred_element_type=f32)
    back_leaf = y_leaf - col_sum(terms)
    x_leaf = row_sum(
        jnp.einsum("gij,gis->gjs", leaf_inv, half16(back_leaf), preferred_element_type=f32)
    )
    return (x_root, x_child[None], x_leaf, y_root)


def solution(mesh):
    in_specs = (
        P("col", None),
        P("layer", "col", None),
        P("layer", "col", None),
        P("row", "col"),
        P("layer", "row", "col"),
        P("layer", "row", "col"),
        P("layer", "col", "row"),
        P("layer", "col", "row"),
        P("layer", "col", "row"),
    )
    out_specs = (P("col", None), P("layer", "col", None), P("layer", "col", None), P("row", None))
    return jax.shard_map(
        on_device, mesh=mesh, in_specs=in_specs, out_specs=out_specs, check_vma=False
    )
```

profile of v0, /device:TPU:2, one launch (start us, length us, event | category | flops | bytes accessed | tf_op | source)
XLA Modules:
  0.0 1495.1 jit_solution(6463682180785090896)
XLA Ops:
  7.2 0.0 copy-start
  7.2 0.0 all-reduce.11.cloned.1.call-start
  7.2 2.5 fusion.18
  9.7 0.0 all-reduce.11.cloned.1.call-update
  9.7 0.0 all-reduce.13.cloned.1.call-start
  9.8 48.8 %all-reduce.11.cloned.1.call-done = f32[2,128,128]{2,1,0:T(8,128)} async-done(((f32[2,128,128]{2,1,0:T(8,128)}), f32[2,128,128]{2,1,0:T(8,128)}) %all-reduce.11.cloned.1.call-update) | async-done | bytes 131088 | tf_op jit(solution)/shard_map/psum | solution.py:8
  58.5 2.6 convolution_bitcast_fusion.2
  61.2 0.0 all-reduce.13.cloned.1.call-update
  61.2 0.0 all-reduce.15.cloned.1.call-start
  61.2 152.3 %all-reduce.13.cloned.1.call-done = f32[2048,128]{1,0:T(8,128)} async-done(((f32[2048,128]{1,0:T(8,128)}), f32[2048,128]{1,0:T(8,128)}) %all-reduce.13.cloned.1.call-update) | async-done | bytes 1048592 | tf_op jit(solution)/shard_map/psum | solution.py:12
  213.5 2.7 convolution_bitcast_fusion.6
  216.2 0.0 all-reduce.15.cloned.1.call-update
  216.3 0.0 all-reduce.17.cloned.1.call-start
  216.3 3.6 convolution_bitcast_fusion
  219.9 38.4 %all-reduce.15.cloned.1.call-done = f32[256,128]{0,1:T(8,128)} async-done(((f32[256,128]{0,1:T(8,128)}), f32[256,128]{0,1:T(8,128)}) %all-reduce.15.cloned.1.call-update) | async-done | bytes 131088 | tf_op jit(solution)/shard_map/psum | solution.py:8
  258.3 3.7 fusion
  262.0 0.0 all-reduce.17.cloned.1.call-update
  262.0 0.0 all-reduce.19.cloned.1.call-start
  262.1 612.7 %all-reduce.17.cloned.1.call-done = f32[4096,128]{1,0:T(8,128)} async-done(((f32[4096,128]{1,0:T(8,128)}), f32[4096,128]{1,0:T(8,128)}) %all-reduce.17.cloned.1.call-update) | async-done | bytes 2097168 | tf_op jit(solution)/shard_map/psum | solution.py:16
  874.8 5.7 convolution_bitcast_fusion.5
  880.5 0.0 all-reduce.19.cloned.1.call-update
  880.6 0.0 all-reduce.21.cloned.1.call-start
  880.6 43.7 %all-reduce.19.cloned.1.call-done = f32[512,128]{0,1:T(8,128)} async-done(((f32[512,128]{0,1:T(8,128)}), f32[512,128]{0,1:T(8,128)}) %all-reduce.19.cloned.1.call-update) | async-done | bytes 262160 | tf_op jit(solution)/shard_map/psum | solution.py:8
  924.4 4.3 convolution_bitcast_fusion.1
  928.7 0.0 all-reduce.21.cloned.1.call-update
  928.7 0.0 all-reduce.23.cloned.1.call-start
  928.8 154.9 %all-reduce.21.cloned.1.call-done = f32[4096,128]{0,1:T(8,128)} async-done(((f32[4096,128]{0,1:T(8,128)}), f32[4096,128]{0,1:T(8,128)}) %all-reduce.21.cloned.1.call-update) | async-done | bytes 2097168 | tf_op jit(solution)/shard_map/psum | solution.py:12
  1083.7 2.7 fusion.4
  1086.4 0.0 all-reduce.23.cloned.1.call-update
  1086.4 0.0 all-reduce.25.cloned.1.call-start
  1086.5 42.2 %all-reduce.23.cloned.1.call-done = f32[256,128]{0,1:T(8,128)} async-done(((f32[256,128]{0,1:T(8,128)}), f32[256,128]{0,1:T(8,128)}) %all-reduce.23.cloned.1.call-update) | async-done | bytes 131088 | tf_op jit(solution)/shard_map/psum | solution.py:8
  1128.7 2.2 convolution_bitcast_fusion.3
  1130.9 0.0 all-reduce.25.cloned.1.call-update
  1130.9 0.0 all-reduce.27.cloned.1.call-start
  1131.0 152.7 %all-reduce.25.cloned.1.call-done = f32[2048,128]{0,1:T(8,128)} async-done(((f32[2048,128]{0,1:T(8,128)}), f32[2048,128]{0,1:T(8,128)}) %all-reduce.25.cloned.1.call-update) | async-done | bytes 1048592 | tf_op jit(solution)/shard_map/psum | solution.py:12
  1283.7 2.2 fusion.13
  1285.9 0.0 copy-start.4
  1285.9 3.1 fusion.7
  1289.1 0.0 all-reduce.27.cloned.1.call-update
  1289.1 0.0 all-reduce.29.cloned.1.call-start
  1289.2 41.6 %all-reduce.27.cloned.1.call-done = f32[2,128,128]{2,1,0:T(8,128)} async-done(((f32[2,128,128]{2,1,0:T(8,128)}), f32[2,128,128]{2,1,0:T(8,128)}) %all-reduce.27.cloned.1.call-update) | async-done | bytes 131088 | tf_op jit(solution)/shard_map/psum | solution.py:8
  1330.8 2.2 convolution_bitcast_fusion.4
  1333.0 0.0 all-reduce.29.cloned.1.call-update
  1333.1 0.8 copy.17
  1333.9 3.0 copy.14
  1336.9 1.3 copy.15
  1338.2 147.5 %all-reduce.29.cloned.1.call-done = f32[2,1024,128]{1,2,0:T(8,128)} async-done(((f32[2,1024,128]{1,2,0:T(8,128)}), f32[2,1024,128]{1,2,0:T(8,128)}) %all-reduce.29.cloned.1.call-update) | async-done | bytes 1048592 | tf_op jit(solution)/shard_map/psum | solution.py:12
  1485.7 2.5 copy.16
  (14 shorter events, 0.0 us)
Async XLA Ops:
  7.2 251.2 %copy-start = (bf16[1,4096,256]{2,1,0:T(8,128)(2,1)S(1)}, bf16[1,4096,256]{2,1,0:T(8,128)(2,1)}, u32[]{:S(2)}) copy-start(bf16[1,4096,256]{2,1,0:T(8,128)(2,1)} %param.17) | copy-start | bytes 6291460
  7.2 51.4 %all-reduce.11.cloned.1.call-start = ((), (), s32[]{:S(2)}) async-start(), calls=%async_computation | async-start | bytes 262144 | tf_op jit(solution)/shard_map/psum | solution.py:8
  9.7 203.8 %copy-start.2 = (bf16[1,256,2048]{2,1,0:T(8,128)(2,1)S(1)}, bf16[1,256,2048]{2,1,0:T(8,128)(2,1)}, u32[]{:S(2)}) copy-start(bf16[1,256,2048]{2,1,0:T(8,128)(2,1)} %param.13) | copy-start | bytes 3145732
  9.7 203.8 %all-reduce.13.cloned.1.call-start = ((), (), s32[]{:S(2)}) async-start(), calls=%async_computation.1 | async-start | bytes 2097152 | tf_op jit(solution)/shard_map/psum | solution.py:12
  61.2 155.1 %copy-start.5 = (f32[2,128,128]{2,1,0:T(8,128)S(1)}, f32[2,128,128]{2,1,0:T(8,128)}, u32[]{:S(2)}) copy-start(f32[2,128,128]{2,1,0:T(8,128)} %all-reduce.11.cloned.1.call-done) | copy-start | bytes 393220
  61.2 197.1 %all-reduce.15.cloned.1.call-start = ((), (), s32[]{:S(2)}) async-start(), calls=%async_computation.2 | async-start | bytes 262144 | tf_op jit(solution)/shard_map/psum | solution.py:8
  216.3 658.6 %all-reduce.17.cloned.1.call-start = ((), (), s32[]{:S(2)}) async-start(), calls=%async_computation.3 | async-start | bytes 4194304 | tf_op jit(solution)/shard_map/psum | solution.py:16
  262.0 662.3 %all-reduce.19.cloned.1.call-start = ((), (), s32[]{:S(2)}) async-start(), calls=%async_computation.4 | async-start | bytes 524288 | tf_op jit(solution)/shard_map/psum | solution.py:8
  880.6 203.1 %all-reduce.21.cloned.1.call-start = ((), (), s32[]{:S(2)}) async-start(), calls=%async_computation.5 | async-start | bytes 4194304 | tf_op jit(solution)/shard_map/psum | solution.py:12
  928.7 200.0 %copy-start.7 = (f32[256,128]{0,1:T(8,128)S(1)}, f32[256,128]{0,1:T(8,128)}, u32[]{:S(2)}) copy-start(f32[256,128]{0,1:T(8,128)} %all-reduce.15.cloned.1.call-done) | copy-start | bytes 393220
  928.7 200.0 %all-reduce.23.cloned.1.call-start = ((), (), s32[]{:S(2)}) async-start(), calls=%async_computation.6 | async-start | bytes 262144 | tf_op jit(solution)/shard_map/psum | solution.py:8
  1086.4 197.3 %all-reduce.25.cloned.1.call-start = ((), (), s32[]{:S(2)}) async-start(), calls=%async_computation.7 | async-start | bytes 2097152 | tf_op jit(solution)/shard_map/psum | solution.py:12
  1130.9 199.9 %all-reduce.27.cloned.1.call-start = ((), (), s32[]{:S(2)}) async-start(), calls=%async_computation.8 | async-start | bytes 262144 | tf_op jit(solution)/shard_map/psum | solution.py:8
  1283.7 2.2 copy-start.1
  1285.9 44.9 %copy-start.4 = (bf16[2,128,1024]{2,1,0:T(8,128)(2,1)S(1)}, bf16[2,128,1024]{2,1,0:T(8,128)(2,1)}, u32[]{:S(2)}) copy-start(bf16[2,128,1024]{2,1,0:T(8,128)(2,1)} %param.14) | copy-start | bytes 1572868
  1289.1 44.0 %copy-start.6 = (f32[512,128]{0,1:T(8,128)S(1)}, f32[512,128]{0,1:T(8,128)}, u32[]{:S(2)}) copy-start(f32[512,128]{0,1:T(8,128)} %all-reduce.19.cloned.1.call-done) | copy-start | bytes 786436
  1289.1 196.6 %all-reduce.29.cloned.1.call-start = ((), (), s32[]{:S(2)}) async-start(), calls=%async_computation.9 | async-start | bytes 2097152 | tf_op jit(solution)/shard_map/psum | solution.py:12
  1333.9 3.0 copy-start.3
Sparse Core Ops, SparseCore 0:
  11.2 47.3 all-reduce.10
  62.6 150.9 all-reduce.12
  216.7 41.5 all-reduce.14
  262.2 612.6 all-reduce.16
  880.7 43.6 all-reduce.18
  928.8 154.8 all-reduce.20
  1086.9 41.7 all-reduce.22
  1132.7 150.9 all-reduce.24
  1289.2 41.5 all-reduce.26
  1334.7 150.9 all-reduce.28
where the time goes:
time: 1500 us
  waiting for transfers between devices  1440 us (96%)
  matrix products  37.6 us (3%)
    psum x1, waiting for transfers between devices, root_total(): return lax.psum(values, ('layer', 'row'))  613 us
    psum x4, waiting for transfers between devices, row_sum(): return lax.psum(values, 'row')  607 us
    psum x5, waiting for transfers between devices, col_sum(): return lax.psum(values, 'col')  215 us
  transfers between devices with their start and end apart: 10, of which 10 were waited for; matrix products, arithmetic and copies ran while one was open for 1% of the time, Pallas kernels for 0%

commit v1 on v0

--- a/solution.py
+++ b/solution.py
@@ -13,7 +13,10 @@
 
 
 def root_total(values):
-    return lax.psum(values, ("layer", "row"))
+    pairs_all_place = lambda local_array, axis_id, which_axis: jax.lax.psum(
+        jax.lax.psum(local_array, axis_id), which_axis
+    )
+    return pairs_all_place(values, "layer", which_axis="row")
 
 
 def half16(values):

time: 1500 us -> 1120 us (0.75)
  waiting for transfers between devices: 1440 us -> 1060 us
    psum x1 -> x2, waiting for transfers between devices: 613 us -> 234 us  [the longest x1 160 us: root_total(): jax.lax.psum(jax.lax.psum(local_array, axis_id), which_axis)]
  transfers between devices with their start and end apart: 10 -> 11, of which waited for: 10 -> 11; matrix products, arithmetic and copies ran while one was open for 1% -> 1% of each run, Pallas kernels for 0% -> 0%
where the time goes in v1:
time: 1120 us; the launch traced here: 1110 us
  waiting for transfers between devices  1060 us (95%)
  matrix products  37.6 us (3%)
  between operations  13.9 us (1%)
    psum x4, waiting for transfers between devices, row_sum(): return lax.psum(values, 'row')  608 us
    psum x5, waiting for transfers between devices, col_sum(): return lax.psum(values, 'col')  214 us
    psum x1, waiting for transfers between devices, root_total(): jax.lax.psum(jax.lax.psum(local_array, axis_id), which_axis)  160 us
    psum x1, waiting for transfers between devices, root_total(): jax.lax.psum(local_array, axis_id)  74.1 us
  transfers between devices with their start and end apart: 11, of which 11 were waited for; matrix products, arithmetic and copies ran while one was open for 1% of the time, Pallas kernels for 0%

profile of v1, /device:TPU:2, one launch (start us, length us, event | category | flops | bytes accessed | tf_op | source)
XLA Modules:
  0.0 1115.0 jit_solution(5426813346997227982)
XLA Ops:
  7.2 0.0 all-reduce.12.cloned.1.call-start
  7.2 2.5 fusion.18
  9.7 0.0 all-reduce.12.cloned.1.call-update
  9.7 0.0 all-reduce.14.cloned.1.call-start
  9.8 48.8 %all-reduce.12.cloned.1.call-done = f32[2,128,128]{2,1,0:T(8,128)} async-done(((f32[2,128,128]{2,1,0:T(8,128)}), f32[2,128,128]{2,1,0:T(8,128)}) %all-reduce.12.cloned.1.call-update) | async-done | bytes 131088 | tf_op jit(solution)/shard_map/psum | solution.py:8
  58.5 2.6 convolution_bitcast_fusion.2
  61.2 0.0 all-reduce.14.cloned.1.call-update
  61.2 0.0 all-reduce.16.cloned.1.call-start
  61.2 152.3 %all-reduce.14.cloned.1.call-done = f32[2048,128]{1,0:T(8,128)} async-done(((f32[2048,128]{1,0:T(8,128)}), f32[2048,128]{1,0:T(8,128)}) %all-reduce.14.cloned.1.call-update) | async-done | bytes 1048592 | tf_op jit(solution)/shard_map/psum | solution.py:12
  213.5 2.7 convolution_bitcast_fusion.6
  216.2 0.0 all-reduce.16.cloned.1.call-update
  216.3 0.0 all-reduce.18.cloned.1.call-start
  216.3 3.6 convolution_bitcast_fusion
  219.9 38.4 %all-reduce.16.cloned.1.call-done = f32[256,128]{0,1:T(8,128)} async-done(((f32[256,128]{0,1:T(8,128)}), f32[256,128]{0,1:T(8,128)}) %all-reduce.16.cloned.1.call-update) | async-done | bytes 131088 | tf_op jit(solution)/shard_map/psum | solution.py:8
  258.3 3.7 fusion
  262.0 0.0 all-reduce.18.cloned.1.call-update
  262.0 0.0 all-reduce.20.cloned.1.call-start
  262.1 74.1 %all-reduce.18.cloned.1.call-done = f32[4096,128]{1,0:T(8,128)} async-done(((f32[4096,128]{1,0:T(8,128)}), f32[4096,128]{1,0:T(8,128)}) %all-reduce.18.cloned.1.call-update) | async-done | bytes 2097168 | tf_op jit(solution)/shard_map/psum | solution.py:17
  336.2 0.0 all-reduce.22.cloned.1.call-start
  336.2 159.9 %all-reduce.20.cloned.1.call-done = f32[4096,128]{1,0:T(8,128)} async-done(((f32[4096,128]{1,0:T(8,128)}), f32[4096,128]{1,0:T(8,128)}) %all-reduce.20.cloned.1.call-update) | async-done | bytes 2097168 | tf_op jit(solution)/shard_map/psum | solution.py:16
  496.1 5.7 convolution_bitcast_fusion.5
  501.8 0.0 all-reduce.22.cloned.1.call-update
  501.8 0.0 all-reduce.24.cloned.1.call-start
  501.9 42.6 %all-reduce.22.cloned.1.call-done = f32[512,128]{0,1:T(8,128)} async-done(((f32[512,128]{0,1:T(8,128)}), f32[512,128]{0,1:T(8,128)}) %all-reduce.22.cloned.1.call-update) | async-done | bytes 262160 | tf_op jit(solution)/shard_map/psum | solution.py:8
  544.4 4.3 convolution_bitcast_fusion.1
  548.8 0.0 all-reduce.24.cloned.1.call-update
  548.8 0.0 all-reduce.26.cloned.1.call-start
  548.8 154.9 %all-reduce.24.cloned.1.call-done = f32[4096,128]{0,1:T(8,128)} async-done(((f32[4096,128]{0,1:T(8,128)}), f32[4096,128]{0,1:T(8,128)}) %all-reduce.24.cloned.1.call-update) | async-done | bytes 2097168 | tf_op jit(solution)/shard_map/psum | solution.py:12
  703.7 2.7 fusion.4
  706.4 0.0 all-reduce.26.cloned.1.call-update
  706.5 0.0 all-reduce.28.cloned.1.call-start
  706.5 42.2 %all-reduce.26.cloned.1.call-done = f32[256,128]{0,1:T(8,128)} async-done(((f32[256,128]{0,1:T(8,128)}), f32[256,128]{0,1:T(8,128)}) %all-reduce.26.cloned.1.call-update) | async-done | bytes 131088 | tf_op jit(solution)/shard_map/psum | solution.py:8
  748.8 2.2 convolution_bitcast_fusion.3
  750.9 0.0 all-reduce.28.cloned.1.call-update
  751.0 0.0 all-reduce.30.cloned.1.call-start
  751.0 152.7 %all-reduce.28.cloned.1.call-done = f32[2048,128]{0,1:T(8,128)} async-done(((f32[2048,128]{0,1:T(8,128)}), f32[2048,128]{0,1:T(8,128)}) %all-reduce.28.cloned.1.call-update) | async-done | bytes 1048592 | tf_op jit(solution)/shard_map/psum | solution.py:12
  903.8 2.2 fusion.13
  906.0 3.1 fusion.7
  909.2 0.0 all-reduce.30.cloned.1.call-update
  909.2 0.0 all-reduce.32.cloned.1.call-start
  909.2 41.6 %all-reduce.30.cloned.1.call-done = f32[2,128,128]{2,1,0:T(8,128)} async-done(((f32[2,128,128]{2,1,0:T(8,128)}), f32[2,128,128]{2,1,0:T(8,128)}) %all-reduce.30.cloned.1.call-update) | async-done | bytes 131088 | tf_op jit(solution)/shard_map/psum | solution.py:8
  950.9 2.2 convolution_bitcast_fusion.4
  953.1 0.0 all-reduce.32.cloned.1.call-update
  953.1 0.8 copy.17
  954.0 3.0 copy.14
  956.9 1.3 copy.15
  958.2 147.7 %all-reduce.32.cloned.1.call-done = f32[2,1024,128]{1,2,0:T(8,128)} async-done(((f32[2,1024,128]{1,2,0:T(8,128)}), f32[2,1024,128]{1,2,0:T(8,128)}) %all-reduce.32.cloned.1.call-update) | async-done | bytes 1048592 | tf_op jit(solution)/shard_map/psum | solution.py:12
  1105.9 2.5 copy.16
  (17 shorter events, 0.1 us)
Async XLA Ops:
  7.2 251.2 %copy-start = (bf16[1,4096,256]{2,1,0:T(8,128)(2,1)S(1)}, bf16[1,4096,256]{2,1,0:T(8,128)(2,1)}, u32[]{:S(2)}) copy-start(bf16[1,4096,256]{2,1,0:T(8,128)(2,1)} %param.17) | copy-start | bytes 6291460
  7.2 51.4 %all-reduce.12.cloned.1.call-start = ((), (), s32[]{:S(2)}) async-start(), calls=%async_computation | async-start | bytes 262144 | tf_op jit(solution)/shard_map/psum | solution.py:8
  9.7 203.8 %copy-start.2 = (bf16[1,256,2048]{2,1,0:T(8,128)(2,1)S(1)}, bf16[1,256,2048]{2,1,0:T(8,128)(2,1)}, u32[]{:S(2)}) copy-start(bf16[1,256,2048]{2,1,0:T(8,128)(2,1)} %param.13) | copy-start | bytes 3145732
  9.7 203.8 %all-reduce.14.cloned.1.call-start = ((), (), s32[]{:S(2)}) async-start(), calls=%async_computation.1 | async-start | bytes 2097152 | tf_op jit(solution)/shard_map/psum | solution.py:12
  61.2 155.1 %copy-start.5 = (f32[2,128,128]{2,1,0:T(8,128)S(1)}, f32[2,128,128]{2,1,0:T(8,128)}, u32[]{:S(2)}) copy-start(f32[2,128,128]{2,1,0:T(8,128)} %all-reduce.12.cloned.1.call-done) | copy-start | bytes 393220
  61.2 197.1 %all-reduce.16.cloned.1.call-start = ((), (), s32[]{:S(2)}) async-start(), calls=%async_computation.2 | async-start | bytes 262144 | tf_op jit(solution)/shard_map/psum | solution.py:8
  216.3 119.9 %all-reduce.18.cloned.1.call-start = ((), (), s32[]{:S(2)}) async-start(), calls=%async_computation.3 | async-start | bytes 4194304 | tf_op jit(solution)/shard_map/psum | solution.py:17
  262.0 234.1 %all-reduce.20.cloned.1.call-start = ((), (), s32[]{:S(2)}) async-start(), calls=%async_computation.4 | async-start | bytes 4194304 | tf_op jit(solution)/shard_map/psum | solution.py:16
  336.2 208.3 %all-reduce.22.cloned.1.call-start = ((), (), s32[]{:S(2)}) async-start(), calls=%async_computation.5 | async-start | bytes 524288 | tf_op jit(solution)/shard_map/psum | solution.py:8
  501.8 201.9 %all-reduce.24.cloned.1.call-start = ((), (), s32[]{:S(2)}) async-start(), calls=%async_computation.6 | async-start | bytes 4194304 | tf_op jit(solution)/shard_map/psum | solution.py:12
  548.8 200.0 %copy-start.7 = (f32[256,128]{0,1:T(8,128)S(1)}, f32[256,128]{0,1:T(8,128)}, u32[]{:S(2)}) copy-start(f32[256,128]{0,1:T(8,128)} %all-reduce.16.cloned.1.call-done) | copy-start | bytes 393220
  548.8 200.0 %all-reduce.26.cloned.1.call-start = ((), (), s32[]{:S(2)}) async-start(), calls=%async_computation.7 | async-start | bytes 262144 | tf_op jit(solution)/shard_map/psum | solution.py:8
  706.5 197.3 %all-reduce.28.cloned.1.call-start = ((), (), s32[]{:S(2)}) async-start(), calls=%async_computation.8 | async-start | bytes 2097152 | tf_op jit(solution)/shard_map/psum | solution.py:12
  751.0 199.9 %all-reduce.30.cloned.1.call-start = ((), (), s32[]{:S(2)}) async-start(), calls=%async_computation.9 | async-start | bytes 262144 | tf_op jit(solution)/shard_map/psum | solution.py:8
  903.8 2.2 copy-start.1
  906.0 44.9 %copy-start.4 = (bf16[2,128,1024]{2,1,0:T(8,128)(2,1)S(1)}, bf16[2,128,1024]{2,1,0:T(8,128)(2,1)}, u32[]{:S(2)}) copy-start(bf16[2,128,1024]{2,1,0:T(8,128)(2,1)} %param.14) | copy-start | bytes 1572868
  909.1 44.0 %copy-start.6 = (f32[512,128]{0,1:T(8,128)S(1)}, f32[512,128]{0,1:T(8,128)}, u32[]{:S(2)}) copy-start(f32[512,128]{0,1:T(8,128)} %all-reduce.22.cloned.1.call-done) | copy-start | bytes 786436
  909.2 196.8 %all-reduce.32.cloned.1.call-start = ((), (), s32[]{:S(2)}) async-start(), calls=%async_computation.10 | async-start | bytes 2097152 | tf_op jit(solution)/shard_map/psum | solution.py:12
  954.0 3.0 copy-start.3
Sparse Core Ops, SparseCore 0:
  11.2 47.3 all-reduce.11
  62.6 150.9 all-reduce.13
  216.7 41.5 all-reduce.15
  262.2 73.9 all-reduce.17
  339.5 156.5 all-reduce.19
  501.9 42.4 all-reduce.21
  548.9 154.8 all-reduce.23
  706.9 41.7 all-reduce.25
  752.8 150.9 all-reduce.27
  909.3 41.5 all-reduce.29
  954.9 150.9 all-reduce.31
